TPU v7x, 256 devices: a whole 4x4x8 slice. The times are simulated.
256 devices in a mesh: grp: 8 (over z), tok: 32 (over y, x, core).
Axes of the slice: x: 4, y: 4, z: 8, core: 2. Of those that a mesh axis runs over, the one named last changes fastest.
Arguments:
- residual_in: bfloat16 [8192, 2048], P(('tok', 'grp')), may hold values from -2.5 to 2.5
- queries: bfloat16 [8192, 2048], P('tok', 'grp'), may hold values from -120 to 120
- fresh_pairs: bfloat16 [8192, 2048], P('tok'), may hold values from -6 to 6
- cache_pairs: bfloat16 [16384, 2048], P('tok'), may hold values from -6 to 6
- segment_ids: int32 [8192], replicated, may hold values from 0 to 15, never falling along the last dimension, each value on 1 to 4096 neighbouring positions
- prefix_length: int32 [16], replicated, may hold values from 0 to 256, as said below
- page_order: int32 [1024], replicated, may hold values from 0 to 1023, each once
- out_weight: bfloat16 [2048, 2048], P('grp'), may hold values from -0.125 to 0.125
- post_gain: float32 [2048], replicated, may hold values from 0.25 to 1.75
- gate_weight: bfloat16 [2048, 4096], P(None, 'grp'), may hold values from -0.125 to 0.125
- up_weight: bfloat16 [2048, 4096], P(None, 'grp'), may hold values from -0.125 to 0.125
- down_weight: bfloat16 [4096, 2048], P('grp'), may hold values from -0.09375 to 0.09375
- next_gain: float32 [2048], replicated, may hold values from 0.25 to 1.75
- next_weight: bfloat16 [2048, 4096], P(None, 'grp'), may hold values from -0.125 to 0.125
Outputs:
- attended: bfloat16 [8192, 2048], P('tok', 'grp')
- new_cache: bfloat16 [16384, 2048], P('tok', 'grp')
- layer_out: bfloat16 [8192, 2048], P(('tok', 'grp'))
- next_proj: bfloat16 [8192, 4096], P('tok', 'grp')
Inputs may be any that keep to these rules, and one draw needn't show every extreme that they name: `segment_ids`: segment numbers never fall along the stream; each of the 16 segments has 1 to 4096 tokens and one has exactly 4096. `prefix_length`: one segment has exactly 256 cached tokens. `page_order`: each page number appears once.
All inputs are finite; a program needn't handle non-finite values.
Results may differ from a plain program's by a relative error of at most 0.024.
Values may be sent and summed in bfloat16 or wider, within the bound.
A program may use at most 128 MiB of HBM per device.

v0:
```python
import math
import jax
import jax.numpy as jnp
from jax import lax
from jax.sharding import PartitionSpec as P

HD = 256
PAGE = 16
masked_score = -1e30
norm_epsilon = 1e-05


def page_tables(segment_ids, prefix_length, page_order, page_rows):
    seg_count = prefix_length.shape[0]
    seg_range = jnp.arange(seg_count, dtype=jnp.int32)
    seg_len = jnp.sum(
        (segment_ids[None, :] == seg_range[:, None]).astype(jnp.int32), axis=1, dtype=jnp.int32
    )
    seg_start = jnp.cumsum(seg_len, dtype=jnp.int32) - seg_len
    needed = (prefix_length + seg_len + page_rows - 1) // page_rows
    cum_end = jnp.cumsum(needed, dtype=jnp.int32)
    first_slot = cum_end - needed
    page_count = page_order.shape[0]
    page_range = jnp.arange(page_count, dtype=jnp.int32)
    ranking = jnp.sum(
        jnp.where(page_order[None, :] == page_range[:, None], page_range[None, :], 0),
        axis=1,
        dtype=jnp.int32,
    )
    owners = jnp.sum(
        (cum_end[None, :] <= ranking[:, None]).astype(jnp.int32), axis=1, dtype=jnp.int32
    )
    onehot = (owners[:, None] == seg_range[None, :]).astype(jnp.int32)
    page_first = (
        ranking - jnp.sum(onehot * first_slot[None, :], axis=1, dtype=jnp.int32)
    ) * page_rows
    page_prefix = jnp.sum(onehot * prefix_length[None, :], axis=1, dtype=jnp.int32)
    page_len = jnp.sum(onehot * seg_len[None, :], axis=1, dtype=jnp.int32)
    page_start = jnp.sum(onehot * seg_start[None, :], axis=1, dtype=jnp.int32)
    return (owners, page_first, page_prefix, page_len, page_start)


def row_info(tables, row_first, count, page_rows):
    sliced = [
        jnp.repeat(
            lax.dynamic_slice_in_dim(table, row_first // page_rows, count // page_rows), page_rows
        )
        for table in tables
    ]
    position = sliced[1] + (row_first + jnp.arange(count, dtype=jnp.int32)) % page_rows
    return (sliced[0], position, sliced[2], sliced[3], sliced[4])


def attend_piece(state, query_four, pairs, visible):
    maxima, totals, weighted = state
    rows_here = pairs.shape[0]
    split = pairs.reshape(rows_here, query_four.shape[1], 2, query_four.shape[3])
    score_scale = 1.0 / math.sqrt(HD)
    scores = (
        jnp.einsum("tkgd,nkd->tkgn", query_four, split[:, :, 0], preferred_element_type=jnp.float32)
        * score_scale
    )
    live = visible[:, None, None, :]
    scores = jnp.where(live, scores, masked_score)
    raised = jnp.maximum(maxima, jnp.max(scores, axis=3))
    weights = jnp.where(live, jnp.exp(scores - raised[..., None]), 0.0)
    rescale = jnp.exp(maxima - raised)
    totals = totals * rescale + jnp.sum(weights, axis=3)
    weighted = weighted * rescale[..., None] + jnp.einsum(
        "tkgn,nkd->tkgd",
        weights.astype(jnp.bfloat16),
        split[:, :, 1],
        preferred_element_type=jnp.float32,
    )
    return (raised, totals, weighted)


def update_state(state, query_four, pairs, visible):
    return attend_piece(state, query_four, pairs, visible)


def empty_state(rows_here, pairs_here, per_pair):
    return (
        jnp.full((rows_here, pairs_here, per_pair), masked_score, jnp.float32),
        jnp.zeros((rows_here, pairs_here, per_pair), jnp.float32),
        jnp.zeros((rows_here, pairs_here, per_pair, HD), jnp.float32),
    )


def rms_scale(rows, gain):
    values = rows.astype(jnp.float32)
    scaled = values * lax.rsqrt(jnp.mean(values * values, axis=-1, keepdims=True) + norm_epsilon)
    return (scaled * gain).astype(jnp.bfloat16)


def local(
    residual_in,
    queries,
    fresh_pairs,
    cache_pairs,
    segment_ids,
    prefix_length,
    page_order,
    out_weight,
    post_gain,
    gate_weight,
    up_weight,
    down_weight,
    next_gain,
    next_weight,
):
    group = lax.axis_index("grp")
    shard = lax.axis_index("tok")
    groups = lax.axis_size("grp")
    tok_rows = queries.shape[0]
    heads_here = queries.shape[1] // HD
    pairs_here = max(1, heads_here // 2)
    per_pair = heads_here // pairs_here
    kv_first = group * heads_here // 2
    width_pairs = pairs_here * 2 * HD
    own_cols = cache_pairs.shape[1] // groups
    own_offset = group * own_cols - kv_first * 2 * HD
    query_four = queries.reshape(tok_rows, pairs_here, per_pair, HD)
    own_first = shard * tok_rows
    own_pos = own_first + jnp.arange(tok_rows, dtype=jnp.int32)
    own_seg = lax.dynamic_slice_in_dim(segment_ids, own_first, tok_rows)
    tables = page_tables(segment_ids, prefix_length, page_order, PAGE)
    cache_rows = cache_pairs.shape[0]
    cache_first = shard * cache_rows
    fresh_mine = lax.dynamic_slice_in_dim(fresh_pairs, kv_first * 2 * HD, width_pairs, 1)
    cache_mine = lax.dynamic_slice_in_dim(cache_pairs, kv_first * 2 * HD, width_pairs, 1)
    cache_info = row_info(tables, cache_first, cache_rows, PAGE)
    portion = lax.all_gather(cache_mine, "tok", axis=0, tiled=True)
    info = row_info(tables, jnp.int32(0), portion.shape[0], PAGE)
    visible = (info[0][None, :] == own_seg[:, None]) & (info[1] < info[2])[None, :]
    state = update_state(empty_state(tok_rows, pairs_here, per_pair), query_four, portion, visible)
    write_live = (cache_info[1] >= cache_info[2]) & (cache_info[1] < cache_info[2] + cache_info[3])
    write_token = cache_info[4] + cache_info[1] - cache_info[2]
    own_cache = lax.dynamic_slice_in_dim(cache_pairs, group * own_cols, own_cols, 1)
    portion = lax.all_gather(fresh_mine, "tok", axis=0, tiled=True)
    current = state
    written = own_cache
    count = portion.shape[0]
    key_pos = jnp.arange(count, dtype=jnp.int32)
    visible = (segment_ids[None, :] == own_seg[:, None]) & (key_pos[None, :] <= own_pos[:, None])
    current = update_state(current, query_four, portion, visible)
    landing = write_live & (write_token >= 0) & (write_token < count)
    mine = lax.dynamic_slice_in_dim(portion, own_offset, own_cols, 1)
    taken = jnp.take(mine, jnp.clip(write_token, 0, count - 1), axis=0)
    written = jnp.where(landing[:, None], taken, written)
    maxima, totals, weighted = current
    attended = (
        (weighted / totals[..., None]).reshape(tok_rows, heads_here * HD).astype(jnp.bfloat16)
    )
    mixed = lax.psum_scatter(
        jnp.dot(attended, out_weight, preferred_element_type=jnp.float32).astype(jnp.bfloat16),
        "grp",
        scatter_dimension=0,
        tiled=True,
    ).astype(jnp.float32)
    first_sum = (residual_in.astype(jnp.float32) + mixed).astype(jnp.bfloat16)
    post_normed = rms_scale(first_sum, post_gain)
    portion = lax.all_gather(post_normed, "grp", axis=0, tiled=True)
    gate = jnp.dot(portion, gate_weight, preferred_element_type=jnp.float32)
    up_part = jnp.dot(portion, up_weight, preferred_element_type=jnp.float32)
    hidden = (jax.nn.silu(gate) * up_part).astype(jnp.bfloat16)
    partial_rows = jnp.dot(hidden, down_weight, preferred_element_type=jnp.float32)
    ffn_out = lax.psum_scatter(
        partial_rows.astype(jnp.bfloat16), "grp", scatter_dimension=0, tiled=True
    ).astype(jnp.float32)
    layer_out = (first_sum.astype(jnp.float32) + ffn_out).astype(jnp.bfloat16)
    next_normed = rms_scale(layer_out, next_gain)
    next_proj = jnp.dot(
        lax.all_gather(next_normed, "grp", axis=0, tiled=True),
        next_weight,
        preferred_element_type=jnp.float32,
    ).astype(jnp.bfloat16)
    return (attended, written, layer_out, next_proj)


def solution(mesh):
    in_specs = (
        P(("tok", "grp"), None),
        P("tok", "grp"),
        P("tok", None),
        P("tok", None),
        P(),
        P(),
        P(),
        P("grp", None),
        P(),
        P(None, "grp"),
        P(None, "grp"),
        P("grp", None),
        P(),
        P(None, "grp"),
    )
    out_specs = (P("tok", "grp"), P("tok", "grp"), P(("tok", "grp"), None), P("tok", "grp"))
    return jax.shard_map(local, mesh=mesh, in_specs=in_specs, out_specs=out_specs, check_vma=False)
```

profile of v0, /device:TPU:2, one launch (start us, length us, event | category | flops | bytes accessed | tf_op | source)
XLA Modules:
  0.0 377.0 jit_solution(1616883388557246644)
XLA Ops:
  7.2 1.8 constant_dynamic-slice_fusion.1
  9.1 1.1 constant_dynamic-slice_fusion.2
  10.2 1.0 copy.42
  11.3 0.8 dynamic_slice.30
  12.1 0.9 convert_reduce_fusion
  14.2 1.2 select_reduce_fusion
  15.5 1.4 select_reduce_fusion.2
  18.1 53.8 %all-gather.7.cloned.1.call-done = bf16[8192,512]{1,0:T(8,128)(2,1)} async-done(((bf16[256,512]{1,0:T(8,128)(2,1)}), bf16[8192,512]{1,0:T(8,128)(2,1)}) %all-gather.7.cloned.1.call-update) | async-done | bytes 8388624 | tf_op jit(solution)/shard_map/all_gather | solution.py:140
  71.9 12.5 %reshape.514 = bf16[8192,1,2,256]{3,2,0,1:T(2,128)(2,1)} reshape(bf16[8192,512]{1,0:T(8,128)(2,1)} %all-gather.7.cloned.1.call-done) | data formatting | bytes 16777216 | tf_op jit(solution)/shard_map/reshape | solution.py:57
  84.4 17.2 %fusion.78 = (bf16[8192,1,1,256]{3,2,0,1:T(2,128)(2,1)}, bf16[8192,1,1,256]{3,2,0,1:T(2,128)(2,1)S(1)}) fusion(bf16[8192,1,2,256]{3,2,0,1:T(2,128)(2,1)} %reshape.514), kind=kLoop, calls=%fused_computation.121 | loop fusion | bytes 16777216 | tf_op jit(solution)/shard_map/slice | solution.py:72
  101.6 7.7 %fusion.81 = (f32[256]{0:T(256)S(1)}, f32[256,1,1,8192]{0,3,2,1:T(8,128)}) fusion(bf16[256,256]{1,0:T(8,128)(2,1)S(1)} %copy-done.9, bf16[8192,1,1,256]{3,2,0,1:T(2,128)(2,1)S(1)} %get-tuple-element.29, s32[256]{0:T(256)S(1)} %iota_add_fusion, s32[256]{0:T(256)S(1)} %dynamic_slice.30, s32[8192]{0:T(1024)S(1)} %copy-done.6), kind=kOutput, calls=%fused_computation.124 | convolution fusion | flops 1086324480 | bytes 12749824 | tf_op jit(solution)/shard_map/tkgd,nkd->tkgn/dot_general | solution.py:60
  109.3 49.4 %all-gather.5.cloned.1.call-done = bf16[16384,512]{0,1:T(8,128)(2,1)} async-done(((bf16[512,512]{0,1:T(8,128)(2,1)}), bf16[16384,512]{0,1:T(8,128)(2,1)}) %all-gather.5.cloned.1.call-update) | async-done | bytes 16777232 | tf_op jit(solution)/shard_map/all_gather | solution.py:133
  158.7 9.8 %fusion.80 = (f32[256]{0:T(256)S(1)}, f32[256,1,1,16384]{0,3,2,1:T(8,128)S(1)}) fusion(bf16[256,256]{1,0:T(8,128)(2,1)S(1)} %copy-done.9, bf16[16384,1,2,256]{0,3,2,1:T(8,128)(2,1)} %bitcast.108, pred[16384]{0:T(1024)(128)(4,1)S(1)} %fusion.62, s32[256]{0:T(256)S(1)} %dynamic_slice.30, s32[16384]{0:T(1024)S(1)} %eq.89), kind=kOutput, calls=%fused_computation.123 | convolution fusion | flops 2168454912 | bytes 25380864 | tf_op jit(solution)/shard_map/tkgd,nkd->tkgn/dot_general | solution.py:60
  168.5 3.9 %fusion.14 = f32[256]{0:T(256)S(1)} fusion(f32[256,1,1,8192]{0,3,2,1:T(8,128)S(1)} %copy-done.1, f32[256]{0:T(256)S(1)} %get-tuple-element.33, s32[256]{0:T(256)S(1)} %iota_add_fusion, s32[256]{0:T(256)S(1)} %dynamic_slice.30, s32[8192]{0:T(1024)S(1)} %copy-done.6), kind=kLoop, calls=%fused_computation.22 | loop fusion | flops 12582656 | bytes 8425472 | tf_op jit(solution)/shard_map/reduce_sum | solution.py:68
  172.4 3.2 fusion.24
  175.7 6.0 %fusion.2 = f32[256]{0:T(256)S(1)} fusion(f32[256,1,1,16384]{0,3,2,1:T(8,128)S(1)} %get-tuple-element.38, f32[256]{0:T(256)S(1)} %get-tuple-element.34, s32[256]{0:T(256)S(1)} %dynamic_slice.30, s32[16384]{0:T(1024)S(1)} %eq.89, pred[16384]{0:T(1024)(128)(4,1)S(1)} %fusion.62), kind=kLoop, calls=%fused_computation.6 | loop fusion | flops 20971264 | bytes 16862208 | tf_op jit(solution)/shard_map/reduce_sum | solution.py:68
  181.7 20.1 %fusion.45 = bf16[256,256]{0,1:T(8,128)(2,1)S(1)} fusion(f32[1,256,256,1]{2,1,3,0:T(8,128)S(1)} %fusion.24, f32[256,1,1,16384]{0,3,2,1:T(8,128)S(1)} %get-tuple-element.38, f32[256]{0:T(256)S(1)} %get-tuple-element.34, s32[256]{0:T(256)S(1)} %dynamic_slice.30, s32[16384]{0:T(1024)S(1)} %eq.89, pred[16384]{0:T(1024)(128)(4,1)S(1)} %fusion.62, ...), kind=kOutput, calls=%fused_computation.46 | convolution fusion | flops 2168782848 | bytes 25646080 | tf_op jit(solution)/shard_map/tkgn,nkd->tkgd/dot_general | solution.py:69
  201.8 1.5 convolution_convert_fusion.1
  203.3 39.7 %reduce-scatter.3.cloned.1.call-done = bf16[32,2048]{1,0:T(8,128)(2,1)} async-done(((bf16[256,2048]{1,0:T(8,128)(2,1)}), bf16[32,2048]{1,0:T(8,128)(2,1)}) %reduce-scatter.3.cloned.1.call-update) | async-done | bytes 131088 | tf_op jit(solution)/shard_map/reduce_scatter | solution.py:155
  243.0 1.1 fusion.56
  244.1 1.7 fusion.58
  246.0 37.0 %all-gather.9.cloned.1.call-done = bf16[256,2048]{1,0:T(8,128)(2,1)} async-done(((bf16[32,2048]{1,0:T(8,128)(2,1)}), bf16[256,2048]{1,0:T(8,128)(2,1)}) %all-gather.9.cloned.1.call-update) | async-done | bytes 1048592 | tf_op jit(solution)/shard_map/all_gather | solution.py:163
  283.0 2.6 fusion.82
  285.6 4.3 %convolution_convert_fusion = bf16[256,2048]{1,0:T(8,128)(2,1)} fusion(bf16[512,2048]{1,0:T(8,128)(2,1)S(1)} %copy-done, bf16[256,2048]{1,0:T(8,128)(2,1)} %all-gather.9.cloned.1.call-done, bf16[2048,512]{1,0:T(8,128)(2,1)} %param.24, f32[256,512]{1,0:T(8,128)S(1)} %fusion.82), kind=kOutput, calls=%fused_computation.34 | convolution fusion | flops 1075052544 | bytes 6815744 | tf_op jit(solution)/shard_map/dot_general | solution.py:167
  290.0 37.5 %reduce-scatter.5.cloned.1.call-done = bf16[32,2048]{1,0:T(8,128)(2,1)} async-done(((bf16[256,2048]{1,0:T(8,128)(2,1)}), bf16[32,2048]{1,0:T(8,128)(2,1)}) %reduce-scatter.5.cloned.1.call-update) | async-done | bytes 131088 | tf_op jit(solution)/shard_map/reduce_scatter | solution.py:168
  327.5 1.1 fusion.53
  330.7 4.4 %constant_dynamic-slice_fusion = bf16[8192,256]{1,0:T(8,128)(2,1)} fusion(bf16[8192,512]{1,0:T(8,128)(2,1)} %all-gather.7.cloned.1.call-done, s32[]{:T(128)S(6)} %select_n.127), kind=kLoop, calls=%fused_computation.111 | loop fusion | bytes 8388612 | tf_op jit(solution)/shard_map/dynamic_slice | solution.py:148
  335.0 4.3 %gather_fusion = bf16[512,256]{1,0:T(8,128)(2,1)S(1)} fusion(bf16[8192,256]{1,0:T(8,128)(2,1)} %constant_dynamic-slice_fusion, s32[1024]{0:T(1024)S(1)} %pad_clamp_fusion), kind=kCustom, calls=%fused_computation | custom fusion | bytes 526336 | tf_op jit(solution)/shard_map/jit(_take)/gather | solution.py:149
  339.3 1.9 dynamic-slice_select_fusion
  341.2 0.8 copy.41
  342.0 24.9 %all-gather.11.cloned.1.call-done = bf16[256,2048]{1,0:T(8,128)(2,1)} async-done(((bf16[32,2048]{1,0:T(8,128)(2,1)}), bf16[256,2048]{1,0:T(8,128)(2,1)}) %all-gather.11.cloned.1.call-update) | async-done | bytes 1048592 | tf_op jit(solution)/shard_map/all_gather | solution.py:174
  366.8 3.3 convolution_convert_fusion.2
  (78 shorter events, 5.0 us)
Async XLA Ops:
  7.2 278.5 %copy-start = (bf16[512,2048]{1,0:T(8,128)(2,1)S(1)}, bf16[512,2048]{1,0:T(8,128)(2,1)}, u32[]{:S(2)}) copy-start(bf16[512,2048]{1,0:T(8,128)(2,1)} %param.25) | copy-start | bytes 6291460
  7.2 64.7 %all-gather.7.cloned.1.call-start = ((), (), s32[]{:S(2)}) async-start(), calls=%async_computation.3 | async-start | bytes 8650752 | tf_op jit(solution)/shard_map/all_gather | solution.py:140
  9.1 149.6 %all-gather.5.cloned.1.call-start = ((), (), s32[]{:S(2)}) async-start(), calls=%async_computation.2 | async-start | bytes 17301504 | tf_op jit(solution)/shard_map/all_gather | solution.py:133
  11.3 231.7 %reduce-scatter.3.cloned.1.call-start = ((), (), s32[]{:S(2)}) async-start(), calls=%async_computation.4 | async-start | bytes 1179648 | tf_op jit(solution)/shard_map/reduce_scatter | solution.py:155
  84.4 17.2 %copy-start.6 = (s32[8192]{0:T(1024)S(1)}, s32[8192]{0:T(1024)}, u32[]{:S(2)}) copy-start(s32[8192]{0:T(1024)} %param.18) | copy-start | bytes 98308
  84.4 17.2 %copy-start.9 = (bf16[256,256]{1,0:T(8,128)(2,1)S(1)}, bf16[256,256]{1,0:T(8,128)(2,1)}, u32[]{:S(2)}) copy-start(bf16[256,256]{1,0:T(8,128)(2,1)} %param.15) | copy-start | bytes 393220
  158.7 13.7 %slice-start = ((s8[8388608]{0:T(1024)(128)(4,1)}), s8[4194304]{0:T(1024)(128)(4,1)S(1)}, s32[]{:S(2)}) async-start(s8[8388608]{0:T(1024)(128)(4,1)} %bitcast.103), calls=%async_computation.8 | async-start | bytes 8388608
  158.7 9.8 %copy-start.1 = (f32[256,1,1,8192]{0,3,2,1:T(8,128)S(1)}, f32[256,1,1,8192]{0,3,2,1:T(8,128)}, u32[]{:S(2)}) copy-start(f32[256,1,1,8192]{0,3,2,1:T(8,128)} %get-tuple-element.40) | copy-start | bytes 25165828
  158.7 13.7 %slice-start.1 = ((s8[8388608]{0:T(1024)(128)(4,1)}), s8[4194304]{0:T(1024)(128)(4,1)S(1)}, s32[]{:S(2)}) async-start(s8[8388608]{0:T(1024)(128)(4,1)} %bitcast.103), calls=%async_computation.9 | async-start | bytes 8388608
  181.6 20.1 %copy-start.4 = (bf16[256,2048]{1,0:T(8,128)(2,1)S(1)}, bf16[256,2048]{1,0:T(8,128)(2,1)}, u32[]{:S(2)}) copy-start(bf16[256,2048]{1,0:T(8,128)(2,1)} %param.21) | copy-start | bytes 3145732
  181.7 61.3 %copy-start.2 = (bf16[32,2048]{1,0:T(8,128)(2,1)S(1)}, bf16[32,2048]{1,0:T(8,128)(2,1)}, u32[]{:S(2)}) copy-start(bf16[32,2048]{1,0:T(8,128)(2,1)} %param.14) | copy-start | bytes 393220
  181.7 62.5 %copy-start.7 = (f32[2048]{0:T(1024)S(1)}, f32[2048]{0:T(1024)}, u32[]{:S(2)}) copy-start(f32[2048]{0:T(1024)} %param.22) | copy-start | bytes 24580
  203.2 125.4 %copy-start.8 = (f32[2048]{0:T(1024)S(1)}, f32[2048]{0:T(1024)}, u32[]{:S(2)}) copy-start(f32[2048]{0:T(1024)} %param.26) | copy-start | bytes 24580
  203.3 79.7 %all-gather.9.cloned.1.call-start = ((), (), s32[]{:S(2)}) async-start(), calls=%async_computation.5 | async-start | bytes 1179648 | tf_op jit(solution)/shard_map/all_gather | solution.py:163
  243.0 84.5 %copy-start.3 = (bf16[32,2048]{1,0:T(8,128)(2,1)S(1)}, bf16[32,2048]{1,0:T(8,128)(2,1)}, u32[]{:S(2)}) copy-start(bf16[32,2048]{1,0:T(8,128)(2,1)} %reduce-scatter.3.cloned.1.call-done) | copy-start | bytes 393220
  245.8 81.7 %reduce-scatter.5.cloned.1.call-start = ((), (), s32[]{:S(2)}) async-start(), calls=%async_computation.6 | async-start | bytes 1179648 | tf_op jit(solution)/shard_map/reduce_scatter | solution.py:168
  289.9 76.9 %all-gather.11.cloned.1.call-start = ((), (), s32[]{:S(2)}) async-start(), calls=%async_computation.7 | async-start | bytes 1179648 | tf_op jit(solution)/shard_map/all_gather | solution.py:174
  328.6 41.6 %copy-start.5 = (bf16[32,2048]{1,0:T(8,128)(2,1)}, bf16[32,2048]{1,0:T(8,128)(2,1)S(1)}, u32[]{:S(2)}) copy-start(bf16[32,2048]{1,0:T(8,128)(2,1)S(1)} %get-tuple-element.25) | copy-start | bytes 393220
Sparse Core Ops, SparseCore 0:
  11.1 60.7 all-gather.6
  74.4 84.2 all-gather.4
  203.4 39.5 reduce-scatter.2
  245.9 37.0 all-gather.8
  290.1 37.3 reduce-scatter.4
  329.7 37.0 all-gather.10
where the time goes:
time: 378 us; the launch traced here: 377 us
  waiting for transfers between devices  242 us (64%)
  matrix products  52.4 us (14%)
  local copies, waits for them, and re-layouts  46.4 us (12%)
  other arithmetic  21.1 us (6%)
  between operations  14.5 us (4%)
    all_gather x1, waiting for transfers between devices, local(): portion = lax.all_gather(fresh_mine, 'tok', axis=0, tiled=True)  53.8 us
    all_gather x1, waiting for transfers between devices, local(): portion = lax.all_gather(cache_mine, 'tok', axis=0, tiled=True)  49.4 us
    reduce_scatter x1, waiting for transfers between devices, local(): lax.psum_scatter(jnp.dot(attended, out_weight, preferred_element_type=jnp...  39.7 us
    reduce_scatter x1, waiting for transfers between devices, local(): lax.psum_scatter(partial_rows.astype(jnp.bfloat16), 'grp', scatter_dimens...  37.5 us
    all_gather x1, waiting for transfers between devices, local(): portion = lax.all_gather(post_normed, 'grp', axis=0, tiled=True)  37 us
    all_gather x1, waiting for transfers between devices, local(): lax.all_gather(next_normed, 'grp', axis=0, tiled=True)  24.9 us
    dot_general x2, matrix products, attend_piece(): jnp.einsum('tkgn,nkd->tkgd', weights.astype(jnp.bfloat16), split[:, :, 1]...  23.3 us
    dot_general x2, matrix products, attend_piece(): jnp.einsum('tkgd,nkd->tkgn', query_four, split[:, :, 0], preferred_elemen...  17.5 us
  transfers between devices with their start and end apart: 6, of which 6 were waited for; matrix products, arithmetic and copies ran while one was open for 16% of the time, Pallas kernels for 0%

commit v1 on v0

--- a/solution.py
+++ b/solution.py
@@ -3,11 +3,34 @@
 import jax.numpy as jnp
 from jax import lax
 from jax.sharding import PartitionSpec as P
+from jax.lax import axis_index, ppermute, psum
 
 HD = 256
 PAGE = 16
 masked_score = -1e30
 norm_epsilon = 1e-05
+
+
+def terms_handle(x0, axis_name):
+    upper, met_up, left_arr = (psum(1, axis_name), axis_index(axis_name), x0.shape[0])
+    row_list = [to_i * upper if nth == 0 else to_i for nth, to_i in enumerate(x0.shape)]
+    z = lax.dynamic_update_slice_in_dim(
+        jnp.zeros(row_list, x0.dtype), x0, met_up * left_arr, axis=0
+    )
+    all_rows = item_now = x0
+    rr = 1
+    while rr < upper // 2 + 1:
+        all_rows = ppermute(all_rows, axis_name, [(nth, (nth + 1) % upper) for nth in range(upper)])
+        z = lax.dynamic_update_slice_in_dim(z, all_rows, (met_up - rr) % upper * left_arr, axis=0)
+        if 2 * rr < upper:
+            item_now = ppermute(
+                item_now, axis_name, [(nth, (nth - 1) % upper) for nth in range(upper)]
+            )
+            z = lax.dynamic_update_slice_in_dim(
+                z, item_now, (met_up + rr) % upper * left_arr, axis=0
+            )
+        rr += 1
+    return z
 
 
 def page_tables(segment_ids, prefix_length, page_order, page_rows):
@@ -171,9 +194,7 @@
     layer_out = (first_sum.astype(jnp.float32) + ffn_out).astype(jnp.bfloat16)
     next_normed = rms_scale(layer_out, next_gain)
     next_proj = jnp.dot(
-        lax.all_gather(next_normed, "grp", axis=0, tiled=True),
-        next_weight,
-        preferred_element_type=jnp.float32,
+        terms_handle(next_normed, "grp"), next_weight, preferred_element_type=jnp.float32
     ).astype(jnp.bfloat16)
     return (attended, written, layer_out, next_proj)
 

time: 378 us -> 367 us (0.971)
  waiting for transfers between devices: 242 us -> 218 us
  starting transfers between devices: 0.43 us -> 10.6 us
  local copies, waits for them, and re-layouts: 46.4 us -> 50.3 us
    all_gather x1 -> x0, waiting for transfers between devices: 24.9 us -> none  [local(): lax.all_gather(next_normed, 'grp', axis=0, tiled=True)]
    ppermute x0 -> x7, waiting for transfers between devices: none -> 10.8 us  [the longest x4 10.8 us: terms_handle(): ppermute(all_rows, axis_name, [(nth, (nth + 1) % upper) for nth in range(...]
    ppermute x0 -> x7, starting transfers between devices: none -> 10.3 us  [the longest x3 9.34 us: terms_handle(): ppermute(item_now, axis_name, [(nth, (nth - 1) % upper) for nth in range(...]
    reduce_scatter x1, waiting for transfers between devices: 37.5 us -> 27.4 us  [local(): lax.psum_scatter(partial_rows.astype(jnp.bfloat16), 'grp', scatter_dimens...]
  transfers between devices with their start and end apart: 6 -> 12, of which waited for: 6 -> 9; matrix products, arithmetic and copies ran while one was open for 16% -> 17% of each run, Pallas kernels for 0% -> 0%
where the time goes in v1:
time: 367 us; the launch traced here: 366 us
  waiting for transfers between devices  218 us (59%)
  matrix products  52.1 us (14%)
  local copies, waits for them, and re-layouts  50.3 us (14%)
  other arithmetic  20.3 us (6%)
  between operations  14.3 us (4%)
  starting transfers between devices  10.6 us (3%)
    all_gather x1, waiting for transfers between devices, local(): portion = lax.all_gather(fresh_mine, 'tok', axis=0, tiled=True)  53.8 us
    all_gather x1, waiting for transfers between devices, local(): portion = lax.all_gather(cache_mine, 'tok', axis=0, tiled=True)  49.4 us
    reduce_scatter x1, waiting for transfers between devices, local(): lax.psum_scatter(jnp.dot(attended, out_weight, preferred_element_type=jnp...  39.7 us
    all_gather x1, waiting for transfers between devices, local(): portion = lax.all_gather(post_normed, 'grp', axis=0, tiled=True)  37 us
    reduce_scatter x1, waiting for transfers between devices, local(): lax.psum_scatter(partial_rows.astype(jnp.bfloat16), 'grp', scatter_dimens...  27.4 us
    dot_general x2, matrix products, attend_piece(): jnp.einsum('tkgn,nkd->tkgd', weights.astype(jnp.bfloat16), split[:, :, 1]...  23.3 us
    dot_general x2, matrix products, attend_piece(): jnp.einsum('tkgd,nkd->tkgn', query_four, split[:, :, 0], preferred_elemen...  17.4 us
    slice x1, local copies, waits for them, and re-layouts, attend_piece(): split[:, :, 1]  17.2 us
  transfers between devices with their start and end apart: 12, of which 9 were waited for; matrix products, arithmetic and copies ran while one was open for 17% of the time, Pallas kernels for 0%

profile of v1, /device:TPU:2, one launch (start us, length us, event | category | flops | bytes accessed | tf_op | source)
XLA Modules:
  0.0 365.8 jit_solution(9299596596377045157)
XLA Ops:
  7.2 1.8 constant_dynamic-slice_fusion.1
  9.1 1.1 constant_dynamic-slice_fusion.2
  14.2 1.2 select_reduce_fusion
  15.5 1.4 select_reduce_fusion.2
  18.1 53.8 %all-gather.6.cloned.1.call-done = bf16[8192,512]{1,0:T(8,128)(2,1)} async-done(((bf16[256,512]{1,0:T(8,128)(2,1)}), bf16[8192,512]{1,0:T(8,128)(2,1)}) %all-gather.6.cloned.1.call-update) | async-done | bytes 8388624 | tf_op jit(solution)/shard_map/all_gather | solution.py:163
  71.9 12.5 %reshape.514 = bf16[8192,1,2,256]{3,2,0,1:T(2,128)(2,1)} reshape(bf16[8192,512]{1,0:T(8,128)(2,1)} %all-gather.6.cloned.1.call-done) | data formatting | bytes 16777216 | tf_op jit(solution)/shard_map/reshape | solution.py:80
  84.4 17.2 %fusion.79 = (bf16[8192,1,1,256]{3,2,0,1:T(2,128)(2,1)}, bf16[8192,1,1,256]{3,2,0,1:T(2,128)(2,1)S(1)}) fusion(bf16[8192,1,2,256]{3,2,0,1:T(2,128)(2,1)} %reshape.514), kind=kLoop, calls=%fused_computation.129 | loop fusion | bytes 16777216 | tf_op jit(solution)/shard_map/slice | solution.py:95
  101.6 7.7 %fusion.82 = (f32[256]{0:T(256)S(1)}, f32[256,1,1,8192]{0,3,2,1:T(8,128)}) fusion(bf16[256,256]{1,0:T(8,128)(2,1)S(1)} %copy-done.10, bf16[8192,1,1,256]{3,2,0,1:T(2,128)(2,1)S(1)} %get-tuple-element.31, s32[256]{0:T(256)S(1)} %iota_add_fusion, s32[256]{0:T(256)S(1)} %dynamic_slice.30, s32[8192]{0:T(1024)S(1)} %copy-done.7), kind=kOutput, calls=%fused_computation.132 | convolution fusion | flops 1086324480 | bytes 12749824 | tf_op jit(solution)/shard_map/tkgd,nkd->tkgn/dot_general | solution.py:83
  109.3 49.4 %all-gather.4.cloned.1.call-done = bf16[16384,512]{0,1:T(8,128)(2,1)} async-done(((bf16[512,512]{0,1:T(8,128)(2,1)}), bf16[16384,512]{0,1:T(8,128)(2,1)}) %all-gather.4.cloned.1.call-update) | async-done | bytes 16777232 | tf_op jit(solution)/shard_map/all_gather | solution.py:156
  158.7 9.7 %fusion.81 = (f32[256]{0:T(256)S(1)}, f32[256,1,1,16384]{0,3,2,1:T(8,128)S(1)}) fusion(bf16[256,256]{1,0:T(8,128)(2,1)S(1)} %copy-done.10, bf16[16384,1,2,256]{0,3,2,1:T(8,128)(2,1)} %bitcast.108, pred[16384]{0:T(1024)(128)(4,1)S(1)} %fusion.62, s32[256]{0:T(256)S(1)} %dynamic_slice.30, s32[16384]{0:T(1024)S(1)} %eq.97), kind=kOutput, calls=%fused_computation.131 | convolution fusion | flops 2168454912 | bytes 25380864 | tf_op jit(solution)/shard_map/tkgd,nkd->tkgn/dot_general | solution.py:83
  168.5 3.9 %fusion.14 = f32[256]{0:T(256)S(1)} fusion(f32[256,1,1,8192]{0,3,2,1:T(8,128)S(1)} %copy-done.1, f32[256]{0:T(256)S(1)} %get-tuple-element.35, s32[256]{0:T(256)S(1)} %iota_add_fusion, s32[256]{0:T(256)S(1)} %dynamic_slice.30, s32[8192]{0:T(1024)S(1)} %copy-done.7), kind=kLoop, calls=%fused_computation.22 | loop fusion | flops 12582656 | bytes 8425472 | tf_op jit(solution)/shard_map/reduce_sum | solution.py:91
  172.4 3.2 fusion.24
  175.6 6.0 %fusion.2 = f32[256]{0:T(256)S(1)} fusion(f32[256,1,1,16384]{0,3,2,1:T(8,128)S(1)} %get-tuple-element.40, f32[256]{0:T(256)S(1)} %get-tuple-element.36, s32[256]{0:T(256)S(1)} %dynamic_slice.30, s32[16384]{0:T(1024)S(1)} %eq.97, pred[16384]{0:T(1024)(128)(4,1)S(1)} %fusion.62), kind=kLoop, calls=%fused_computation.6 | loop fusion | flops 20971264 | bytes 16862208 | tf_op jit(solution)/shard_map/reduce_sum | solution.py:91
  181.6 20.1 %fusion.45 = bf16[256,256]{0,1:T(8,128)(2,1)S(1)} fusion(f32[1,256,256,1]{2,1,3,0:T(8,128)S(1)} %fusion.24, f32[256,1,1,16384]{0,3,2,1:T(8,128)S(1)} %get-tuple-element.40, f32[256]{0:T(256)S(1)} %get-tuple-element.36, s32[256]{0:T(256)S(1)} %dynamic_slice.30, s32[16384]{0:T(1024)S(1)} %eq.97, pred[16384]{0:T(1024)(128)(4,1)S(1)} %fusion.62, ...), kind=kOutput, calls=%fused_computation.46 | convolution fusion | flops 2168782848 | bytes 25646080 | tf_op jit(solution)/shard_map/tkgn,nkd->tkgd/dot_general | solution.py:92
  202.4 1.4 convolution_convert_fusion.1
  203.9 39.7 %reduce-scatter.3.cloned.1.call-done = bf16[32,2048]{1,0:T(8,128)(2,1)} async-done(((bf16[256,2048]{1,0:T(8,128)(2,1)}), bf16[32,2048]{1,0:T(8,128)(2,1)}) %reduce-scatter.3.cloned.1.call-update) | async-done | bytes 131088 | tf_op jit(solution)/shard_map/reduce_scatter | solution.py:178
  244.7 1.7 fusion.58
  246.6 37.0 %all-gather.8.cloned.1.call-done = bf16[256,2048]{1,0:T(8,128)(2,1)} async-done(((bf16[32,2048]{1,0:T(8,128)(2,1)}), bf16[256,2048]{1,0:T(8,128)(2,1)}) %all-gather.8.cloned.1.call-update) | async-done | bytes 1048592 | tf_op jit(solution)/shard_map/all_gather | solution.py:186
  283.6 2.6 fusion.83
  286.2 4.3 %convolution_convert_fusion = bf16[256,2048]{1,0:T(8,128)(2,1)} fusion(bf16[512,2048]{1,0:T(8,128)(2,1)S(1)} %copy-done, bf16[256,2048]{1,0:T(8,128)(2,1)} %all-gather.8.cloned.1.call-done, bf16[2048,512]{1,0:T(8,128)(2,1)} %param.24, f32[256,512]{1,0:T(8,128)S(1)} %fusion.83), kind=kOutput, calls=%fused_computation.34 | convolution fusion | flops 1075052544 | bytes 6815744 | tf_op jit(solution)/shard_map/dot_general | solution.py:190
  292.0 4.4 %constant_dynamic-slice_fusion = bf16[8192,256]{1,0:T(8,128)(2,1)} fusion(bf16[8192,512]{1,0:T(8,128)(2,1)} %all-gather.6.cloned.1.call-done, s32[]{:T(128)S(6)} %select_n.181), kind=kLoop, calls=%fused_computation.100 | loop fusion | bytes 8388612 | tf_op jit(solution)/shard_map/dynamic_slice | solution.py:171
  296.3 4.3 %gather_fusion = bf16[512,256]{1,0:T(8,128)(2,1)S(1)} fusion(bf16[8192,256]{1,0:T(8,128)(2,1)} %constant_dynamic-slice_fusion, s32[1024]{0:T(1024)S(1)} %pad_clamp_fusion), kind=kCustom, calls=%fused_computation | custom fusion | bytes 526336 | tf_op jit(solution)/shard_map/jit(_take)/gather | solution.py:172
  300.6 27.4 %reduce-scatter.5.cloned.1.call-done = bf16[32,2048]{1,0:T(8,128)(2,1)} async-done(((bf16[256,2048]{1,0:T(8,128)(2,1)}), bf16[32,2048]{1,0:T(8,128)(2,1)}) %reduce-scatter.5.cloned.1.call-update) | async-done | bytes 131088 | tf_op jit(solution)/shard_map/reduce_scatter | solution.py:191
  330.7 2.3 collective-permute-start.1
  333.0 1.9 dynamic-slice_select_fusion
  334.9 1.7 copy.41
  337.2 3.5 collective-permute-start.3
  342.5 1.4 collective-permute-done.2
  343.9 3.5 collective-permute-start.5
  347.5 2.6 collective-permute-done.4
  350.1 6.1 %collective-permute-done.6 = bf16[32,2048]{1,0:T(8,128)(2,1)S(1)} collective-permute-done((bf16[32,2048]{1,0:T(8,128)(2,1)S(1)}, bf16[32,2048]{1,0:T(8,128)(2,1)S(1)}, u32[]{:S(2)}, u32[]{:S(2)}) %collective-permute-start.6) | collective-permute-done | bytes 131104 | tf_op jit(solution)/shard_map/ppermute | solution.py:23
  356.3 3.0 convolution_convert_fusion.2
  (99 shorter events, 13.8 us)
Async XLA Ops:
  7.2 279.0 %copy-start = (bf16[512,2048]{1,0:T(8,128)(2,1)S(1)}, bf16[512,2048]{1,0:T(8,128)(2,1)}, u32[]{:S(2)}) copy-start(bf16[512,2048]{1,0:T(8,128)(2,1)} %param.25) | copy-start | bytes 6291460
  7.2 64.7 %all-gather.6.cloned.1.call-start = ((), (), s32[]{:S(2)}) async-start(), calls=%async_computation.3 | async-start | bytes 8650752 | tf_op jit(solution)/shard_map/all_gather | solution.py:163
  9.1 149.6 %all-gather.4.cloned.1.call-start = ((), (), s32[]{:S(2)}) async-start(), calls=%async_computation.2 | async-start | bytes 17301504 | tf_op jit(solution)/shard_map/all_gather | solution.py:156
  11.3 232.4 %reduce-scatter.3.cloned.1.call-start = ((), (), s32[]{:S(2)}) async-start(), calls=%async_computation.4 | async-start | bytes 1179648 | tf_op jit(solution)/shard_map/reduce_scatter | solution.py:178
  84.4 17.2 %copy-start.7 = (s32[8192]{0:T(1024)S(1)}, s32[8192]{0:T(1024)}, u32[]{:S(2)}) copy-start(s32[8192]{0:T(1024)} %param.18) | copy-start | bytes 98308
  84.4 17.2 %copy-start.10 = (bf16[256,256]{1,0:T(8,128)(2,1)S(1)}, bf16[256,256]{1,0:T(8,128)(2,1)}, u32[]{:S(2)}) copy-start(bf16[256,256]{1,0:T(8,128)(2,1)} %param.15) | copy-start | bytes 393220
  158.7 13.7 %slice-start = ((s8[8388608]{0:T(1024)(128)(4,1)}), s8[4194304]{0:T(1024)(128)(4,1)S(1)}, s32[]{:S(2)}) async-start(s8[8388608]{0:T(1024)(128)(4,1)} %bitcast.103), calls=%async_computation.7 | async-start | bytes 8388608
  158.7 9.8 %copy-start.1 = (f32[256,1,1,8192]{0,3,2,1:T(8,128)S(1)}, f32[256,1,1,8192]{0,3,2,1:T(8,128)}, u32[]{:S(2)}) copy-start(f32[256,1,1,8192]{0,3,2,1:T(8,128)} %get-tuple-element.42) | copy-start | bytes 25165828
  158.7 13.7 %slice-start.1 = ((s8[8388608]{0:T(1024)(128)(4,1)}), s8[4194304]{0:T(1024)(128)(4,1)S(1)}, s32[]{:S(2)}) async-start(s8[8388608]{0:T(1024)(128)(4,1)} %bitcast.103), calls=%async_computation.8 | async-start | bytes 8388608
  181.6 20.8 %copy-start.4 = (bf16[256,2048]{1,0:T(8,128)(2,1)S(1)}, bf16[256,2048]{1,0:T(8,128)(2,1)}, u32[]{:S(2)}) copy-start(bf16[256,2048]{1,0:T(8,128)(2,1)} %param.21) | copy-start | bytes 3145732
  181.6 62.0 %copy-start.2 = (bf16[32,2048]{1,0:T(8,128)(2,1)S(1)}, bf16[32,2048]{1,0:T(8,128)(2,1)}, u32[]{:S(2)}) copy-start(bf16[32,2048]{1,0:T(8,128)(2,1)} %param.14) | copy-start | bytes 393220
  181.6 63.1 %copy-start.8 = (f32[2048]{0:T(1024)S(1)}, f32[2048]{0:T(1024)}, u32[]{:S(2)}) copy-start(f32[2048]{0:T(1024)} %param.22) | copy-start | bytes 24580
  201.7 0.7 copy-start.6
  203.8 79.7 %all-gather.8.cloned.1.call-start = ((), (), s32[]{:S(2)}) async-start(), calls=%async_computation.5 | async-start | bytes 1179648 | tf_op jit(solution)/shard_map/all_gather | solution.py:186
  246.4 81.7 %reduce-scatter.5.cloned.1.call-start = ((), (), s32[]{:S(2)}) async-start(), calls=%async_computation.6 | async-start | bytes 1179648 | tf_op jit(solution)/shard_map/reduce_scatter | solution.py:191
  286.2 41.8 %copy-start.3 = (bf16[32,2048]{1,0:T(8,128)(2,1)S(1)}, bf16[32,2048]{1,0:T(8,128)(2,1)}, u32[]{:S(2)}) copy-start(bf16[32,2048]{1,0:T(8,128)(2,1)} %reduce-scatter.3.cloned.1.call-done) | copy-start | bytes 393220
  290.5 38.8 %copy-start.9 = (f32[2048]{0:T(1024)S(1)}, f32[2048]{0:T(1024)}, u32[]{:S(2)}) copy-start(f32[2048]{0:T(1024)} %param.26) | copy-start | bytes 24580
  329.1 0.7 copy-start.5
  329.8 7.4 %collective-permute-start = (bf16[32,2048]{1,0:T(8,128)(2,1)S(1)}, bf16[32,2048]{1,0:T(8,128)(2,1)}, u32[]{:S(2)}, u32[]{:S(2)}) collective-permute-start(bf16[32,2048]{1,0:T(8,128)(2,1)S(1)} %get-tuple-element.25), channel_id=1, source_target_pairs={{0,32},{32,64},{64,96},{96,128},{128,160},{160,192},{192,224},{224... | collective-permute-start | bytes 393224 | tf_op jit(solution)/shard_map/ppermute | solution.py:23
  330.7 6.5 %collective-permute-start.1 = (bf16[32,2048]{1,0:T(8,128)(2,1)S(1)}, bf16[32,2048]{1,0:T(8,128)(2,1)}, u32[]{:S(2)}, u32[]{:S(2)}) collective-permute-start(bf16[32,2048]{1,0:T(8,128)(2,1)S(1)} %get-tuple-element.25), channel_id=1, source_target_pairs={{0,224},{32,0},{64,32},{96,64},{128,96},{160,128},{192,160},{224,1... | collective-permute-start | bytes 393224 | tf_op jit(solution)/shard_map/ppermute | solution.py:26
  337.2 6.7 %collective-permute-start.2 = (bf16[32,2048]{1,0:T(8,128)(2,1)}, bf16[32,2048]{1,0:T(8,128)(2,1)S(1)}, u32[]{:S(2)}, u32[]{:S(2)}) collective-permute-start(bf16[32,2048]{1,0:T(8,128)(2,1)} %collective-permute-done), channel_id=1, source_target_pairs={{0,32},{32,64},{64,96},{96,128},{128,160},{160,192},{192,224},{224... | collective-permute-start | bytes 393224 | tf_op jit(solution)/shard_map/ppermute | solution.py:23
  337.2 6.7 %collective-permute-start.3 = (bf16[32,2048]{1,0:T(8,128)(2,1)}, bf16[32,2048]{1,0:T(8,128)(2,1)S(1)}, u32[]{:S(2)}, u32[]{:S(2)}) collective-permute-start(bf16[32,2048]{1,0:T(8,128)(2,1)} %collective-permute-done.1), channel_id=1, source_target_pairs={{0,224},{32,0},{64,32},{96,64},{128,96},{160,128},{192,160},{224,1... | collective-permute-start | bytes 393224 | tf_op jit(solution)/shard_map/ppermute | solution.py:26
  343.9 6.2 %collective-permute-start.4 = (bf16[32,2048]{1,0:T(8,128)(2,1)S(1)}, bf16[32,2048]{1,0:T(8,128)(2,1)S(1)}, u32[]{:S(2)}, u32[]{:S(2)}) collective-permute-start(bf16[32,2048]{1,0:T(8,128)(2,1)S(1)} %collective-permute-done.2), channel_id=1, source_target_pairs={{0,32},{32,64},{64,96},{96,128},{128,160},{160,192},{192,224},{224... | collective-permute-start | bytes 393224 | tf_op jit(solution)/shard_map/ppermute | solution.py:23
  343.9 6.2 %collective-permute-start.5 = (bf16[32,2048]{1,0:T(8,128)(2,1)S(1)}, bf16[32,2048]{1,0:T(8,128)(2,1)S(1)}, u32[]{:S(2)}, u32[]{:S(2)}) collective-permute-start(bf16[32,2048]{1,0:T(8,128)(2,1)S(1)} %collective-permute-done.3), channel_id=1, source_target_pairs={{0,224},{32,0},{64,32},{96,64},{128,96},{160,128},{192,160},{224,1... | collective-permute-start | bytes 393224 | tf_op jit(solution)/shard_map/ppermute | solution.py:26
  350.1 6.2 %collective-permute-start.6 = (bf16[32,2048]{1,0:T(8,128)(2,1)S(1)}, bf16[32,2048]{1,0:T(8,128)(2,1)S(1)}, u32[]{:S(2)}, u32[]{:S(2)}) collective-permute-start(bf16[32,2048]{1,0:T(8,128)(2,1)S(1)} %collective-permute-done.4), channel_id=1, source_target_pairs={{0,32},{32,64},{64,96},{96,128},{128,160},{160,192},{192,224},{224... | collective-permute-start | bytes 393224 | tf_op jit(solution)/shard_map/ppermute | solution.py:23
Sparse Core Ops, SparseCore 0:
  11.1 60.7 all-gather.5
  74.4 84.2 all-gather.3
  204.0 39.6 reduce-scatter.2
  246.5 37.0 all-gather.7
  290.7 37.3 reduce-scatter.4
